TPU v7x, 128 devices: a whole 4x4x4 slice. The times are simulated.
128 devices in a mesh: batch: 4 (over z_hi, core), ctx: 32 (over z_lo, y, x).
Axes of the slice: x: 4, y: 4, z: 4 (z_hi: 2, z_lo: 2; z = z_hi * 2 + z_lo), core: 2. Of those that a mesh axis runs over, the one named last changes fastest.
Arguments:
- lengths: int32 [64], P('batch'), parts along dimension 0, may hold values from 1 to 8704, 16384 in all
- queries: bfloat16 [65536, 512], P(('batch', 'ctx')), parts along dimension 0, may hold values from -256 to 256
- key_rows: bfloat16 [65536, 128], P(('batch', 'ctx')), parts along dimension 0, may hold values from -4.5 to 4.5
- values: bfloat16 [65536, 128], P(('batch', 'ctx')), parts along dimension 0, may hold values from -6 to 6
Outputs:
- attended: bfloat16 [65536, 512], P(('batch', 'ctx')), parts along dimension 0
- log_mass: float32 [4, 65536], P(None, ('batch', 'ctx')), parts along dimension 1
There are 4 independent parts, one for each index of `batch`. A program takes and returns all parts, laid end to end along the dimension named above; each array names one. Nothing has to cross between parts.
Inputs may be any that keep to these rules, and one draw needn't show every extreme that they name: The lengths sum to 16384; the longest is exactly 8704.
All inputs are finite; a program needn't handle non-finite values.
Results may differ from a plain program's by a relative error of at most 0.0035.
Values may be sent and summed in bfloat16 or wider, within the bound.
A program may use at most 64 MiB of HBM per device.

v0:
```python
import math

import jax
import jax.numpy as jnp
from jax import lax
from jax.sharding import PartitionSpec as P

QH = 4
HD = 128


def doc_numbers(doc_ends, positions):
    return jnp.sum((positions[:, None] >= doc_ends[None, :]).astype(jnp.int32), axis=1)


def on_device(lengths, queries, key_rows, values):
    q_rows = queries.shape[0]
    quarter = q_rows // 4
    here = lax.axis_index("ctx")
    doc_ends = jnp.cumsum(lengths)
    own_first = here * q_rows
    q_pos = own_first + jnp.arange(q_rows, dtype=jnp.int32)
    score_scale = 1.0 / math.sqrt(HD)

    def make_absorb(set_heads, set_pos, set_live):
        set_doc = doc_numbers(doc_ends, set_pos)
        set_rows = set_pos.shape[0]

        def absorb(running, shard_part, first_row):
            piece_rows = shard_part.shape[1]
            block_rows = math.gcd(piece_rows, 512)

            def absorb_block(block_index, carried):
                offset = block_index * block_rows
                key_block = lax.dynamic_slice_in_dim(shard_part[0], offset, block_rows, 0)
                value_block = lax.dynamic_slice_in_dim(shard_part[1], offset, block_rows, 0)
                k_pos = offset + jnp.arange(block_rows, dtype=jnp.int32)
                k_doc = doc_numbers(doc_ends, k_pos)

                def per_query(query_index, state_all):
                    row_start = query_index * quarter
                    part_heads = lax.dynamic_slice_in_dim(set_heads, row_start, quarter, 0)
                    part_pos = lax.dynamic_slice_in_dim(set_pos, row_start, quarter, 0)
                    part_doc = lax.dynamic_slice_in_dim(set_doc, row_start, quarter, 0)
                    part_live = lax.dynamic_slice_in_dim(set_live, row_start, quarter, 0)
                    visible = (
                        (part_doc[:, None] == k_doc[None, :])
                        & (k_pos[None, :] <= part_pos[:, None])
                        & (k_pos[None, :] >= 0)
                        & part_live[:, None]
                    )
                    run_max = lax.dynamic_slice_in_dim(state_all[0], row_start, quarter, 1)
                    run_sum = lax.dynamic_slice_in_dim(state_all[1], row_start, quarter, 1)
                    run_acc = lax.dynamic_slice_in_dim(state_all[2], row_start, quarter, 1)
                    scores = (
                        jnp.einsum(
                            "thd,kd->htk", part_heads, key_block, preferred_element_type=jnp.float32
                        )
                        * score_scale
                    )
                    scores = jnp.where(visible[None], scores, -1e30)
                    new_max = jnp.maximum(run_max, jnp.max(scores, axis=2))
                    weights = jnp.where(visible[None], jnp.exp(scores - new_max[:, :, None]), 0.0)
                    rescale = jnp.exp(run_max - new_max)
                    new_sum = run_sum * rescale + jnp.sum(weights, axis=2)
                    mixed = jnp.einsum(
                        "htk,kd->htd",
                        weights.astype(jnp.bfloat16),
                        value_block,
                        preferred_element_type=jnp.float32,
                    )
                    new_acc = run_acc * rescale[:, :, None] + mixed
                    return (
                        lax.dynamic_update_slice_in_dim(state_all[0], new_max, row_start, 1),
                        lax.dynamic_update_slice_in_dim(state_all[1], new_sum, row_start, 1),
                        lax.dynamic_update_slice_in_dim(state_all[2], new_acc, row_start, 1),
                    )

                return lax.fori_loop(0, set_rows // quarter, per_query, carried)

            return lax.fori_loop(0, piece_rows // block_rows, absorb_block, running)

        return absorb

    own_heads = queries.reshape(q_rows, QH, HD)
    own_live = jnp.ones((q_rows,), bool)
    stacked = jnp.stack([key_rows, values])
    absorb = make_absorb(own_heads, q_pos, own_live)
    carried_state = absorb(
        (
            jnp.full((QH, q_rows), -1e30, jnp.float32),
            jnp.zeros((QH, q_rows), jnp.float32),
            jnp.zeros((QH, q_rows, HD), jnp.float32),
        ),
        lax.all_gather(stacked, "ctx", axis=1, tiled=True),
        jnp.int32(0),
    )
    run_max, run_sum, run_acc = carried_state
    safe_sum = jnp.where(run_sum > 0.0, run_sum, 1.0)
    mixed = run_acc / safe_sum[:, :, None]
    attended = (
        jnp.transpose(mixed, (1, 0, 2)).reshape(run_max.shape[1], QH * HD).astype(jnp.bfloat16)
    )
    return (attended, run_max + jnp.log(safe_sum))


def solution(mesh):
    in_specs = (
        P("batch"),
        P(("batch", "ctx"), None),
        P(("batch", "ctx"), None),
        P(("batch", "ctx"), None),
    )
    out_specs = (P(("batch", "ctx"), None), P(None, ("batch", "ctx")))
    return jax.shard_map(
        on_device, mesh=mesh, in_specs=in_specs, out_specs=out_specs, check_vma=False
    )
```

profile of v0, /device:TPU:96, one launch (start us, length us, event | category | flops | bytes accessed | tf_op | source)
XLA Modules:
  0.0 505.8 jit_solution(6846417126769314705)
XLA Ops:
  11.5 166.0 %all-gather.2.cloned.1.call-done = bf16[2,16384,128]{2,1,0:T(8,128)(2,1)} async-done(((bf16[2,512,128]{2,1,0:T(8,128)(2,1)}), bf16[2,16384,128]{2,1,0:T(8,128)(2,1)}) %all-gather.2.cloned.1.call-update) | async-done | bytes 8388624 | tf_op jit(solution)/shard_map/all_gather | solution.py:95
  177.5 319.7 %while.52 = (s32[]{:T(128)}, f32[4,512]{1,0:T(4,128)S(1)}, f32[4,512]{1,0:T(4,128)S(1)}, f32[4,512,128]{2,1,0:T(8,128)S(1)}, s32[16]{0:T(128)S(1)}, /*index=5*/b...) while((s32[]{:T(128)}, f32[4,512]{1,0:T(4,128)S(1)}, ...), condition=%wide.region_8.9_spmd.clone, body=%wide.region_2.8_spmd.clone.sunk | while | flops 136997888 | bytes 21709424 | solution.py:81
  177.5 3.8 fusion.30
  181.4 6.0 %while.53 = (s32[]{:T(128)}, f32[4,512]{1,0:T(4,128)S(1)}, f32[4,512]{1,0:T(4,128)S(1)}, f32[4,512,128]{2,1,0:T(8,128)S(1)}, s32[512]{0:T(512)S(1)}, /*index=5*/...) while((s32[]{:T(128)}, f32[4,512]{1,0:T(4,128)S(1)}, ...), condition=%wide.region_7.7_spmd.clone, body=%wide.region_4.6_spmd.clone.sunk | while | flops 136972800 | bytes 4399323 | solution.py:79
  187.5 3.8 fusion.30
  191.4 6.0 %while.53 = (s32[]{:T(128)}, f32[4,512]{1,0:T(4,128)S(1)}, f32[4,512]{1,0:T(4,128)S(1)}, f32[4,512,128]{2,1,0:T(8,128)S(1)}, s32[512]{0:T(512)S(1)}, /*index=5*/...) while((s32[]{:T(128)}, f32[4,512]{1,0:T(4,128)S(1)}, ...), condition=%wide.region_7.7_spmd.clone, body=%wide.region_4.6_spmd.clone.sunk | while | flops 136972800 | bytes 4399323 | solution.py:79
  197.5 3.8 fusion.30
  201.4 6.0 %while.53 = (s32[]{:T(128)}, f32[4,512]{1,0:T(4,128)S(1)}, f32[4,512]{1,0:T(4,128)S(1)}, f32[4,512,128]{2,1,0:T(8,128)S(1)}, s32[512]{0:T(512)S(1)}, /*index=5*/...) while((s32[]{:T(128)}, f32[4,512]{1,0:T(4,128)S(1)}, ...), condition=%wide.region_7.7_spmd.clone, body=%wide.region_4.6_spmd.clone.sunk | while | flops 136972800 | bytes 4399323 | solution.py:79
  207.5 3.8 fusion.30
  211.4 6.0 %while.53 = (s32[]{:T(128)}, f32[4,512]{1,0:T(4,128)S(1)}, f32[4,512]{1,0:T(4,128)S(1)}, f32[4,512,128]{2,1,0:T(8,128)S(1)}, s32[512]{0:T(512)S(1)}, /*index=5*/...) while((s32[]{:T(128)}, f32[4,512]{1,0:T(4,128)S(1)}, ...), condition=%wide.region_7.7_spmd.clone, body=%wide.region_4.6_spmd.clone.sunk | while | flops 136972800 | bytes 4399323 | solution.py:79
  217.5 3.8 fusion.30
  221.4 6.0 %while.53 = (s32[]{:T(128)}, f32[4,512]{1,0:T(4,128)S(1)}, f32[4,512]{1,0:T(4,128)S(1)}, f32[4,512,128]{2,1,0:T(8,128)S(1)}, s32[512]{0:T(512)S(1)}, /*index=5*/...) while((s32[]{:T(128)}, f32[4,512]{1,0:T(4,128)S(1)}, ...), condition=%wide.region_7.7_spmd.clone, body=%wide.region_4.6_spmd.clone.sunk | while | flops 136972800 | bytes 4399323 | solution.py:79
  227.5 3.8 fusion.30
  231.4 6.0 %while.53 = (s32[]{:T(128)}, f32[4,512]{1,0:T(4,128)S(1)}, f32[4,512]{1,0:T(4,128)S(1)}, f32[4,512,128]{2,1,0:T(8,128)S(1)}, s32[512]{0:T(512)S(1)}, /*index=5*/...) while((s32[]{:T(128)}, f32[4,512]{1,0:T(4,128)S(1)}, ...), condition=%wide.region_7.7_spmd.clone, body=%wide.region_4.6_spmd.clone.sunk | while | flops 136972800 | bytes 4399323 | solution.py:79
  237.5 3.8 fusion.30
  241.4 6.0 %while.53 = (s32[]{:T(128)}, f32[4,512]{1,0:T(4,128)S(1)}, f32[4,512]{1,0:T(4,128)S(1)}, f32[4,512,128]{2,1,0:T(8,128)S(1)}, s32[512]{0:T(512)S(1)}, /*index=5*/...) while((s32[]{:T(128)}, f32[4,512]{1,0:T(4,128)S(1)}, ...), condition=%wide.region_7.7_spmd.clone, body=%wide.region_4.6_spmd.clone.sunk | while | flops 136972800 | bytes 4399323 | solution.py:79
  247.5 3.8 fusion.30
  251.4 6.0 %while.53 = (s32[]{:T(128)}, f32[4,512]{1,0:T(4,128)S(1)}, f32[4,512]{1,0:T(4,128)S(1)}, f32[4,512,128]{2,1,0:T(8,128)S(1)}, s32[512]{0:T(512)S(1)}, /*index=5*/...) while((s32[]{:T(128)}, f32[4,512]{1,0:T(4,128)S(1)}, ...), condition=%wide.region_7.7_spmd.clone, body=%wide.region_4.6_spmd.clone.sunk | while | flops 136972800 | bytes 4399323 | solution.py:79
  257.5 3.8 fusion.30
  261.4 6.0 %while.53 = (s32[]{:T(128)}, f32[4,512]{1,0:T(4,128)S(1)}, f32[4,512]{1,0:T(4,128)S(1)}, f32[4,512,128]{2,1,0:T(8,128)S(1)}, s32[512]{0:T(512)S(1)}, /*index=5*/...) while((s32[]{:T(128)}, f32[4,512]{1,0:T(4,128)S(1)}, ...), condition=%wide.region_7.7_spmd.clone, body=%wide.region_4.6_spmd.clone.sunk | while | flops 136972800 | bytes 4399323 | solution.py:79
  267.4 3.8 fusion.30
  271.4 6.0 %while.53 = (s32[]{:T(128)}, f32[4,512]{1,0:T(4,128)S(1)}, f32[4,512]{1,0:T(4,128)S(1)}, f32[4,512,128]{2,1,0:T(8,128)S(1)}, s32[512]{0:T(512)S(1)}, /*index=5*/...) while((s32[]{:T(128)}, f32[4,512]{1,0:T(4,128)S(1)}, ...), condition=%wide.region_7.7_spmd.clone, body=%wide.region_4.6_spmd.clone.sunk | while | flops 136972800 | bytes 4399323 | solution.py:79
  277.4 3.8 fusion.30
  281.3 6.0 %while.53 = (s32[]{:T(128)}, f32[4,512]{1,0:T(4,128)S(1)}, f32[4,512]{1,0:T(4,128)S(1)}, f32[4,512,128]{2,1,0:T(8,128)S(1)}, s32[512]{0:T(512)S(1)}, /*index=5*/...) while((s32[]{:T(128)}, f32[4,512]{1,0:T(4,128)S(1)}, ...), condition=%wide.region_7.7_spmd.clone, body=%wide.region_4.6_spmd.clone.sunk | while | flops 136972800 | bytes 4399323 | solution.py:79
  287.4 3.8 fusion.30
  291.3 6.0 %while.53 = (s32[]{:T(128)}, f32[4,512]{1,0:T(4,128)S(1)}, f32[4,512]{1,0:T(4,128)S(1)}, f32[4,512,128]{2,1,0:T(8,128)S(1)}, s32[512]{0:T(512)S(1)}, /*index=5*/...) while((s32[]{:T(128)}, f32[4,512]{1,0:T(4,128)S(1)}, ...), condition=%wide.region_7.7_spmd.clone, body=%wide.region_4.6_spmd.clone.sunk | while | flops 136972800 | bytes 4399323 | solution.py:79
  297.4 3.8 fusion.30
  301.3 6.0 %while.53 = (s32[]{:T(128)}, f32[4,512]{1,0:T(4,128)S(1)}, f32[4,512]{1,0:T(4,128)S(1)}, f32[4,512,128]{2,1,0:T(8,128)S(1)}, s32[512]{0:T(512)S(1)}, /*index=5*/...) while((s32[]{:T(128)}, f32[4,512]{1,0:T(4,128)S(1)}, ...), condition=%wide.region_7.7_spmd.clone, body=%wide.region_4.6_spmd.clone.sunk | while | flops 136972800 | bytes 4399323 | solution.py:79
  307.4 3.8 fusion.30
  311.3 6.0 %while.53 = (s32[]{:T(128)}, f32[4,512]{1,0:T(4,128)S(1)}, f32[4,512]{1,0:T(4,128)S(1)}, f32[4,512,128]{2,1,0:T(8,128)S(1)}, s32[512]{0:T(512)S(1)}, /*index=5*/...) while((s32[]{:T(128)}, f32[4,512]{1,0:T(4,128)S(1)}, ...), condition=%wide.region_7.7_spmd.clone, body=%wide.region_4.6_spmd.clone.sunk | while | flops 136972800 | bytes 4399323 | solution.py:79
  317.4 3.8 fusion.30
  321.3 6.0 %while.53 = (s32[]{:T(128)}, f32[4,512]{1,0:T(4,128)S(1)}, f32[4,512]{1,0:T(4,128)S(1)}, f32[4,512,128]{2,1,0:T(8,128)S(1)}, s32[512]{0:T(512)S(1)}, /*index=5*/...) while((s32[]{:T(128)}, f32[4,512]{1,0:T(4,128)S(1)}, ...), condition=%wide.region_7.7_spmd.clone, body=%wide.region_4.6_spmd.clone.sunk | while | flops 136972800 | bytes 4399323 | solution.py:79
  327.4 3.8 fusion.30
  331.3 6.0 %while.53 = (s32[]{:T(128)}, f32[4,512]{1,0:T(4,128)S(1)}, f32[4,512]{1,0:T(4,128)S(1)}, f32[4,512,128]{2,1,0:T(8,128)S(1)}, s32[512]{0:T(512)S(1)}, /*index=5*/...) while((s32[]{:T(128)}, f32[4,512]{1,0:T(4,128)S(1)}, ...), condition=%wide.region_7.7_spmd.clone, body=%wide.region_4.6_spmd.clone.sunk | while | flops 136972800 | bytes 4399323 | solution.py:79
  337.4 3.8 fusion.30
  341.3 6.0 %while.53 = (s32[]{:T(128)}, f32[4,512]{1,0:T(4,128)S(1)}, f32[4,512]{1,0:T(4,128)S(1)}, f32[4,512,128]{2,1,0:T(8,128)S(1)}, s32[512]{0:T(512)S(1)}, /*index=5*/...) while((s32[]{:T(128)}, f32[4,512]{1,0:T(4,128)S(1)}, ...), condition=%wide.region_7.7_spmd.clone, body=%wide.region_4.6_spmd.clone.sunk | while | flops 136972800 | bytes 4399323 | solution.py:79
  347.4 3.8 fusion.30
  351.3 6.0 %while.53 = (s32[]{:T(128)}, f32[4,512]{1,0:T(4,128)S(1)}, f32[4,512]{1,0:T(4,128)S(1)}, f32[4,512,128]{2,1,0:T(8,128)S(1)}, s32[512]{0:T(512)S(1)}, /*index=5*/...) while((s32[]{:T(128)}, f32[4,512]{1,0:T(4,128)S(1)}, ...), condition=%wide.region_7.7_spmd.clone, body=%wide.region_4.6_spmd.clone.sunk | while | flops 136972800 | bytes 4399323 | solution.py:79
  357.4 3.8 fusion.30
  361.3 6.0 %while.53 = (s32[]{:T(128)}, f32[4,512]{1,0:T(4,128)S(1)}, f32[4,512]{1,0:T(4,128)S(1)}, f32[4,512,128]{2,1,0:T(8,128)S(1)}, s32[512]{0:T(512)S(1)}, /*index=5*/...) while((s32[]{:T(128)}, f32[4,512]{1,0:T(4,128)S(1)}, ...), condition=%wide.region_7.7_spmd.clone, body=%wide.region_4.6_spmd.clone.sunk | while | flops 136972800 | bytes 4399323 | solution.py:79
  367.3 3.8 fusion.30
  371.3 6.0 %while.53 = (s32[]{:T(128)}, f32[4,512]{1,0:T(4,128)S(1)}, f32[4,512]{1,0:T(4,128)S(1)}, f32[4,512,128]{2,1,0:T(8,128)S(1)}, s32[512]{0:T(512)S(1)}, /*index=5*/...) while((s32[]{:T(128)}, f32[4,512]{1,0:T(4,128)S(1)}, ...), condition=%wide.region_7.7_spmd.clone, body=%wide.region_4.6_spmd.clone.sunk | while | flops 136972800 | bytes 4399323 | solution.py:79
  377.3 3.8 fusion.30
  381.2 6.0 %while.53 = (s32[]{:T(128)}, f32[4,512]{1,0:T(4,128)S(1)}, f32[4,512]{1,0:T(4,128)S(1)}, f32[4,512,128]{2,1,0:T(8,128)S(1)}, s32[512]{0:T(512)S(1)}, /*index=5*/...) while((s32[]{:T(128)}, f32[4,512]{1,0:T(4,128)S(1)}, ...), condition=%wide.region_7.7_spmd.clone, body=%wide.region_4.6_spmd.clone.sunk | while | flops 136972800 | bytes 4399323 | solution.py:79
  387.3 3.8 fusion.30
  391.2 6.0 %while.53 = (s32[]{:T(128)}, f32[4,512]{1,0:T(4,128)S(1)}, f32[4,512]{1,0:T(4,128)S(1)}, f32[4,512,128]{2,1,0:T(8,128)S(1)}, s32[512]{0:T(512)S(1)}, /*index=5*/...) while((s32[]{:T(128)}, f32[4,512]{1,0:T(4,128)S(1)}, ...), condition=%wide.region_7.7_spmd.clone, body=%wide.region_4.6_spmd.clone.sunk | while | flops 136972800 | bytes 4399323 | solution.py:79
  397.3 3.8 fusion.30
  401.2 6.0 %while.53 = (s32[]{:T(128)}, f32[4,512]{1,0:T(4,128)S(1)}, f32[4,512]{1,0:T(4,128)S(1)}, f32[4,512,128]{2,1,0:T(8,128)S(1)}, s32[512]{0:T(512)S(1)}, /*index=5*/...) while((s32[]{:T(128)}, f32[4,512]{1,0:T(4,128)S(1)}, ...), condition=%wide.region_7.7_spmd.clone, body=%wide.region_4.6_spmd.clone.sunk | while | flops 136972800 | bytes 4399323 | solution.py:79
  407.3 3.8 fusion.30
  411.2 6.0 %while.53 = (s32[]{:T(128)}, f32[4,512]{1,0:T(4,128)S(1)}, f32[4,512]{1,0:T(4,128)S(1)}, f32[4,512,128]{2,1,0:T(8,128)S(1)}, s32[512]{0:T(512)S(1)}, /*index=5*/...) while((s32[]{:T(128)}, f32[4,512]{1,0:T(4,128)S(1)}, ...), condition=%wide.region_7.7_spmd.clone, body=%wide.region_4.6_spmd.clone.sunk | while | flops 136972800 | bytes 4399323 | solution.py:79
  417.3 3.8 fusion.30
  421.2 6.0 %while.53 = (s32[]{:T(128)}, f32[4,512]{1,0:T(4,128)S(1)}, f32[4,512]{1,0:T(4,128)S(1)}, f32[4,512,128]{2,1,0:T(8,128)S(1)}, s32[512]{0:T(512)S(1)}, /*index=5*/...) while((s32[]{:T(128)}, f32[4,512]{1,0:T(4,128)S(1)}, ...), condition=%wide.region_7.7_spmd.clone, body=%wide.region_4.6_spmd.clone.sunk | while | flops 136972800 | bytes 4399323 | solution.py:79
  427.3 3.8 fusion.30
  431.2 6.0 %while.53 = (s32[]{:T(128)}, f32[4,512]{1,0:T(4,128)S(1)}, f32[4,512]{1,0:T(4,128)S(1)}, f32[4,512,128]{2,1,0:T(8,128)S(1)}, s32[512]{0:T(512)S(1)}, /*index=5*/...) while((s32[]{:T(128)}, f32[4,512]{1,0:T(4,128)S(1)}, ...), condition=%wide.region_7.7_spmd.clone, body=%wide.region_4.6_spmd.clone.sunk | while | flops 136972800 | bytes 4399323 | solution.py:79
  437.3 3.8 fusion.30
  441.2 6.0 %while.53 = (s32[]{:T(128)}, f32[4,512]{1,0:T(4,128)S(1)}, f32[4,512]{1,0:T(4,128)S(1)}, f32[4,512,128]{2,1,0:T(8,128)S(1)}, s32[512]{0:T(512)S(1)}, /*index=5*/...) while((s32[]{:T(128)}, f32[4,512]{1,0:T(4,128)S(1)}, ...), condition=%wide.region_7.7_spmd.clone, body=%wide.region_4.6_spmd.clone.sunk | while | flops 136972800 | bytes 4399323 | solution.py:79
  447.3 3.8 fusion.30
  451.2 6.0 %while.53 = (s32[]{:T(128)}, f32[4,512]{1,0:T(4,128)S(1)}, f32[4,512]{1,0:T(4,128)S(1)}, f32[4,512,128]{2,1,0:T(8,128)S(1)}, s32[512]{0:T(512)S(1)}, /*index=5*/...) while((s32[]{:T(128)}, f32[4,512]{1,0:T(4,128)S(1)}, ...), condition=%wide.region_7.7_spmd.clone, body=%wide.region_4.6_spmd.clone.sunk | while | flops 136972800 | bytes 4399323 | solution.py:79
  457.3 3.8 fusion.30
  461.2 6.0 %while.53 = (s32[]{:T(128)}, f32[4,512]{1,0:T(4,128)S(1)}, f32[4,512]{1,0:T(4,128)S(1)}, f32[4,512,128]{2,1,0:T(8,128)S(1)}, s32[512]{0:T(512)S(1)}, /*index=5*/...) while((s32[]{:T(128)}, f32[4,512]{1,0:T(4,128)S(1)}, ...), condition=%wide.region_7.7_spmd.clone, body=%wide.region_4.6_spmd.clone.sunk | while | flops 136972800 | bytes 4399323 | solution.py:79
  467.2 3.8 fusion.30
  471.2 6.0 %while.53 = (s32[]{:T(128)}, f32[4,512]{1,0:T(4,128)S(1)}, f32[4,512]{1,0:T(4,128)S(1)}, f32[4,512,128]{2,1,0:T(8,128)S(1)}, s32[512]{0:T(512)S(1)}, /*index=5*/...) while((s32[]{:T(128)}, f32[4,512]{1,0:T(4,128)S(1)}, ...), condition=%wide.region_7.7_spmd.clone, body=%wide.region_4.6_spmd.clone.sunk | while | flops 136972800 | bytes 4399323 | solution.py:79
  481.1 6.0 %while.53 = (s32[]{:T(128)}, f32[4,512]{1,0:T(4,128)S(1)}, f32[4,512]{1,0:T(4,128)S(1)}, f32[4,512,128]{2,1,0:T(8,128)S(1)}, s32[512]{0:T(512)S(1)}, /*index=5*/...) while((s32[]{:T(128)}, f32[4,512]{1,0:T(4,128)S(1)}, ...), condition=%wide.region_7.7_spmd.clone, body=%wide.region_4.6_spmd.clone.sunk | while | flops 136972800 | bytes 4399323 | solution.py:79
  491.1 6.0 %while.53 = (s32[]{:T(128)}, f32[4,512]{1,0:T(4,128)S(1)}, f32[4,512]{1,0:T(4,128)S(1)}, f32[4,512,128]{2,1,0:T(8,128)S(1)}, s32[512]{0:T(512)S(1)}, /*index=5*/...) while((s32[]{:T(128)}, f32[4,512]{1,0:T(4,128)S(1)}, ...), condition=%wide.region_7.7_spmd.clone, body=%wide.region_4.6_spmd.clone.sunk | while | flops 136972800 | bytes 4399323 | solution.py:79
  (1681 shorter events, 204.4 us)
Async XLA Ops:
  7.2 170.3 %all-gather.2.cloned.1.call-start = ((), (), s32[]{:S(2)}) async-start(), calls=%async_computation | async-start | bytes 8650752 | tf_op jit(solution)/shard_map/all_gather | solution.py:95
Sparse Core Ops, SparseCore 0:
  10.2 167.1 all-gather.1
where the time goes:
time: 508 us; the launch traced here: 506 us
  waiting for transfers between devices  166 us (33%)
  local copies, waits for them, and re-layouts  144 us (28%)
  matrix products  100 us (20%)
  other arithmetic  73.8 us (15%)
  between operations  14.1 us (3%)
  loops' own time  8.29 us (2%)
    all_gather x1, waiting for transfers between devices, on_device(): lax.all_gather(stacked, 'ctx', axis=1, tiled=True)  166 us
    slice x32, local copies, waits for them, and re-layouts, absorb_block(): value_block = lax.dynamic_slice_in_dim(shard_part[1], offset, block_rows, 0)  121 us
    dot_general x128, matrix products, per_query(): jnp.einsum('thd,kd->htk', part_heads, key_block, preferred_element_type=j...  51 us
    dot_general x128, matrix products, per_query(): jnp.einsum('htk,kd->htd', weights.astype(jnp.bfloat16), value_block, pref...  49 us
    reduce_sum x128, other arithmetic, per_query(): new_sum = run_sum * rescale + jnp.sum(weights, axis=2)  44.3 us
    and x128, other arithmetic, per_query(): (part_doc[:, None] == k_doc[None, :]) & (k_pos[None, :] <= part_pos[:, No...  16.6 us
  transfers between devices with their start and end apart: 1, of which 1 were waited for; matrix products, arithmetic and copies ran while one was open for 0% of the time, Pallas kernels for 0%

commit v1 on v0

v1 whole, which is shorter than its diff:
```python
import math

import jax
import jax.numpy as jnp
from jax import lax
from jax.experimental import pallas as pl
from jax.experimental.pallas import tpu as pltpu
from jax.sharding import PartitionSpec as P

QH = 4
HD = 128
DOCS = 16
ROWS = 512
PAIR = 2 * ROWS
CHUNK = 512
STRIP = 64
FAR = 1 << 20
HIDE = float(2**20)
SCALE = 1.0 / math.sqrt(HD)
TO_TWO = SCALE / math.log(2.0)
MESH = pl.DeviceIdType.MESH

SWAP, PRED, OWN = 0, 16, 17
SLOT = {
    (3, 0): 1,
    (0, 3): 2,
    (3, 3): 3,
    (1, 0): 4,
    (0, 1): 5,
    (2, 0): 6,
    (3, 1): 7,
    (1, 3): 8,
    (2, 3): 9,
    (1, 1): 10,
    (2, 1): 11,
    (0, 2): 12,
    (3, 2): 13,
    (1, 2): 14,
    (2, 2): 15,
}
AT = {slot: column for column, slot in SLOT.items()}
SENDS = 18


def body(lengths, queries, keys, values, attended, log_mass, kv, qa, acc, top, scores, weights, feats, docs, local, sent, got):
    here = lax.axis_index("ctx")
    z, y, x = here // 16, here // 4 % 4, here % 4
    at_x = lambda to: z * 16 + y * 4 + to % 4
    at_y = lambda to: z * 16 + to % 4 * 4 + x
    left, right, up, down = at_x(x + 3), at_x(x + 1), at_y(y + 3), at_y(y + 1)
    other = (1 - z) * 16 + y * 4 + x

    own_copies = [
        pltpu.make_async_copy(keys, kv.at[OWN // 2, 0, pl.ds(ROWS, ROWS)], local.at[0]),
        pltpu.make_async_copy(values, kv.at[OWN // 2, 1, pl.ds(ROWS, ROWS)], local.at[1]),
    ]
    for copy in own_copies:
        copy.start()
    barrier = pltpu.get_barrier_semaphore()
    for neighbour in (left, right, up, down, other):
        pl.semaphore_signal(barrier, inc=1, device_id={"ctx": neighbour}, device_id_type=MESH)
    pl.semaphore_wait(barrier, 5)
    for copy in own_copies:
        copy.wait()

    def held(slot):
        return kv.at[slot // 2, :, pl.ds(slot % 2 * ROWS, ROWS)]

    def push(number, source, slot, to):
        return pltpu.make_async_remote_copy(
            src_ref=held(source),
            dst_ref=held(slot),
            send_sem=sent.at[number],
            recv_sem=got.at[slot],
            device_id={"ctx": to},
            device_id_type=MESH,
        )

    def arrive(slot):
        push(0, OWN, slot, other).wait_recv()

    firsts = (
        (1, SLOT[0, 3], right, x < 3),
        (2, SLOT[0, 1], left, x == 0),
        (3, SLOT[3, 0], down, y < 3),
        (4, SLOT[1, 0], up, y == 0),
    )
    middle_x = (x == 1) | (x == 2)
    middle_y = (y == 1) | (y == 2)

    push(0, OWN, SWAP, other).start()
    for number, slot, to, later in firsts:

        @pl.when(later | (z == 0))
        def _():
            push(number, OWN, slot, to).start()

    lane = lax.broadcasted_iota(jnp.int32, (8, 128), 1)
    begins, ends = jnp.full((8, 128), FAR, jnp.int32), jnp.zeros((8, 128), jnp.int32)
    total = jnp.int32(0)
    for doc in range(DOCS):
        begins = jnp.where(lane == doc, total, begins)
        total = total + lengths[doc]
        ends = jnp.where(lane == doc, total, ends)
    docs[0:8] = begins
    docs[8:16] = ends

    def inside(first):
        place = first + lax.broadcasted_iota(jnp.int32, (ROWS, 128), 0)
        return (place >= docs[0:1]) & (place < docs[8:9])

    hide = jnp.where(inside(here * ROWS), -HIDE, 0.0).astype(jnp.bfloat16)
    for head in range(QH):
        qa[head * ROWS : (head + 1) * ROWS, 0:HD] = queries[:, head * HD : (head + 1) * HD]
        qa[head * ROWS : (head + 1) * ROWS, HD:] = hide
    top[...] = jnp.full(top.shape, -1e30, jnp.float32)
    acc[...] = jnp.zeros(acc.shape, jnp.float32)

    def attend(pair, half, width, reach):
        where = pl.ds(half * ROWS, width)
        key_part = jnp.concatenate([kv[pair, 0, where], feats[where]], 1)
        value_part = jnp.concatenate([kv[pair, 1, where], jnp.ones((width, HD), jnp.bfloat16)], 1)
        chunks = QH * ROWS // CHUNK

        def score(chunk):
            scores[chunk % 2, :, 0:width] = lax.dot_general(
                qa[chunk * CHUNK : (chunk + 1) * CHUNK],
                key_part,
                (((1,), (1,)), ((), ())),
                preferred_element_type=jnp.float32,
            )

        def soften(chunk):
            for strip in range(CHUNK // STRIP):
                at = slice(strip * STRIP, (strip + 1) * STRIP)
                rows = slice(chunk * CHUNK + strip * STRIP, chunk * CHUNK + (strip + 1) * STRIP)
                raw = scores[chunk % 2, at, 0:width]
                if reach is not None:
                    row = rows.start % ROWS + lax.broadcasted_iota(jnp.int32, raw.shape, 0)
                    raw = jnp.where(lax.broadcasted_iota(jnp.int32, raw.shape, 1) <= row + reach, raw, -1e30)
                parts = [raw[:, j : j + 128] for j in range(0, width, 128)]
                most = parts[0]
                for part in parts[1:]:
                    most = jnp.maximum(most, part)
                most = jnp.broadcast_to(jnp.max(most, axis=1, keepdims=True), (STRIP, 128))
                before = top[rows]
                now = jnp.maximum(before, most)
                fade = jnp.exp2((before - now) * TO_TWO)
                acc[rows] = acc[rows] * jnp.concatenate([fade, fade], 1)
                top[rows] = now
                for j, part in enumerate(parts):
                    weights[chunk % 2, at, j * 128 : (j + 1) * 128] = jnp.exp2((part - now) * TO_TWO).astype(
                        jnp.bfloat16
                    )

        def mix(chunk):
            rows = slice(chunk * CHUNK, (chunk + 1) * CHUNK)
            acc[rows] = acc[rows] + jnp.dot(
                weights[chunk % 2, :, 0:width], value_part, preferred_element_type=jnp.float32
            )

        score(0)
        for chunk in range(chunks):
            if chunk + 1 < chunks:
                score(chunk + 1)
            if chunk > 0:
                mix(chunk - 1)
            soften(chunk)
        mix(chunks - 1)

    def first_of(slot):
        if slot == OWN:
            return here * ROWS
        if slot == PRED:
            return jnp.where((z == 1) & (here > 16), (here - 17) * ROWS, FAR)
        if slot == SWAP:
            return jnp.where(z == 1, (here - 16) * ROWS, FAR)
        dy, dx = AT[slot]
        column = (y + dy) % 4 * 4 + (x + dx) % 4
        before = column < here % 16
        return jnp.where(before, z * 16 + column, jnp.where(z == 1, column, FAR // ROWS)) * ROWS

    def look(slot):
        feats[pl.ds(slot % 2 * ROWS, ROWS)] = jnp.where(inside(first_of(slot)), 0.0, 1.0).astype(jnp.bfloat16)

    def onward(slot, number):
        dy, _ = AT[slot]
        push(number, slot, SLOT[dy, 3], right).start()
        push(number + 1, slot, SLOT[dy, 1], left).start()

    def relay(slot, number):
        dy, dx = AT[slot]
        to = right if dx == 3 else left

        @pl.when(middle_x if dy in (0, 1) else ~middle_x)
        def _():
            push(number, slot, SLOT[dy, 2], to).start()

    def before_pair(pair):
        for slot in (2 * pair, 2 * pair + 1):
            arrive(slot)
            if slot == SWAP:
                for number, there, to, later in firsts:

                    @pl.when(~(later | (z == 0)))
                    def _():
                        push(number, SWAP, there, to).start()

            elif slot == SLOT[3, 0]:
                onward(slot, 5)

                @pl.when(middle_y)
                def _():
                    push(11, SLOT[3, 0], SLOT[2, 0], down).start()

            elif slot == SLOT[1, 0]:
                onward(slot, 7)

                @pl.when(middle_y)
                def _():
                    push(12, SLOT[1, 0], SLOT[2, 0], up).start()

            elif slot == SLOT[2, 0]:
                onward(slot, 9)
            elif AT[slot][1] == 3:
                relay(slot, 13 if AT[slot][0] in (0, 3) else 14)
            elif AT[slot][1] == 1:
                relay(slot, 15 if AT[slot][0] in (0, 3) else 16)
            look(slot)
        if pair == 1:
            push(17, jnp.where(x > 0, SLOT[0, 3], SLOT[3, 3]), PRED, other).start()

    def step(number, nothing):
        single = (number == 0) | (number == 7)
        pair = jnp.where(number > 7, number - 2, number - 1)
        for which in range(8):

            @pl.when(~single & (pair == which))
            def _():
                before_pair(which)

        @pl.when(number == 0)
        def _():
            look(OWN)

        @pl.when(number == 7)
        def _():
            arrive(PRED)
            look(PRED)

        @pl.when(single)
        def _():
            half = jnp.where(number == 0, 1, 0)
            attend(OWN // 2, pl.multiple_of(half, 1), ROWS, jnp.where(number == 0, 0, ROWS))

        @pl.when(~single)
        def _():
            attend(pair, 0, PAIR, None)

        return nothing

    lax.fori_loop(0, 10, step, 0)

    for head in range(QH):
        rows = slice(head * ROWS, (head + 1) * ROWS)
        mass = acc[rows, HD : HD + 1]
        attended[:, head * HD : (head + 1) * HD] = (acc[rows, 0:HD] / mass).astype(jnp.bfloat16)
        log_mass[head : head + 1, :] = (top[rows, 0:1] * SCALE + jnp.log(mass)).reshape(1, ROWS)

    for number in range(SENDS):
        if number in (11, 12):

            @pl.when(middle_y)
            def _():
                push(number, OWN, SWAP, other).wait_send()

        else:
            push(number, OWN, SWAP, other).wait_send()


def on_device(lengths, queries, key_rows, values):
    vmem = pl.BlockSpec(memory_space=pltpu.VMEM)
    return pl.pallas_call(
        body,
        out_shape=(
            jax.ShapeDtypeStruct((ROWS, QH * HD), jnp.bfloat16),
            jax.ShapeDtypeStruct((QH, ROWS), jnp.float32),
        ),
        in_specs=[
            pl.BlockSpec(memory_space=pltpu.SMEM),
            vmem,
            pl.BlockSpec(memory_space=pl.ANY),
            pl.BlockSpec(memory_space=pl.ANY),
        ],
        out_specs=(vmem, vmem),
        scratch_shapes=[
            pltpu.VMEM((9, 2, PAIR, HD), jnp.bfloat16),
            pltpu.VMEM((QH * ROWS, 2 * HD), jnp.bfloat16),
            pltpu.VMEM((QH * ROWS, 2 * HD), jnp.float32),
            pltpu.VMEM((QH * ROWS, HD), jnp.float32),
            pltpu.VMEM((2, CHUNK, PAIR), jnp.float32),
            pltpu.VMEM((2, CHUNK, PAIR), jnp.bfloat16),
            pltpu.VMEM((PAIR, HD), jnp.bfloat16),
            pltpu.VMEM((16, 128), jnp.int32),
            pltpu.SemaphoreType.DMA((2,)),
            pltpu.SemaphoreType.DMA((SENDS,)),
            pltpu.SemaphoreType.DMA((OWN,)),
        ],
        compiler_params=pltpu.CompilerParams(collective_id=0, has_side_effects=True, vmem_limit_bytes=56 << 20),
    )(lengths, queries, key_rows, values)


def solution(mesh):
    in_specs = (
        P("batch"),
        P(("batch", "ctx"), None),
        P(("batch", "ctx"), None),
        P(("batch", "ctx"), None),
    )
    out_specs = (P(("batch", "ctx"), None), P(None, ("batch", "ctx")))
    step = jax.shard_map(on_device, mesh=mesh, in_specs=in_specs, out_specs=out_specs, check_vma=False)

    def run(*args):
        with jax.sharding.use_abstract_mesh(mesh.abstract_mesh):
            return step(*args)

    return run
```

time: 508 us -> 65.2 us (0.13)
  the two profiles are of different devices: /device:TPU:96 before, /device:TPU:34 now
where the time goes in v1:
time: 65.2 us; the launch traced here: 65 us
  Pallas kernels  61.9 us (95%)
  local copies, waits for them, and re-layouts  2.48 us (4%)
    pallas_call x1, Pallas kernels, on_device(): pl.pallas_call(body, out_shape=(jax.ShapeDtypeStruct((ROWS, QH * HD), jnp...  61.9 us
    unnamed x4, local copies, waits for them, and re-layouts  2.48 us

profile of v1, /device:TPU:34, one launch (start us, length us, event | category | flops | bytes accessed | tf_op | source)
XLA Modules:
  0.0 65.0 jit_solution(11547484669362339873)
XLA Ops:
  0.6 61.9 %shard_map.59 = (bf16[512,512]{1,0:T(8,128)(2,1)}, f32[4,512]{1,0:T(4,128)}) custom-call(s32[16]{0:T(128)} %lengths.1, bf16[512,512]{1,0:T(8,128)(2,1)} %queries.1, bf16[512,128]{1,0:T(8,128)(2,1)} %keys.1, bf16[512,128]{1,0:T(8,128)(2,1)} %values.1), custom_call_target="tpu_custom_call" | custom-call | tf_op jit(solution)/shard_map/pallas_call | solution.py:283
  62.5 0.0 copy-start
  62.5 1.9 %copy.8 = bf16[512,512]{1,0:T(8,128)(2,1)} copy(bf16[512,512]{1,0:T(8,128)(2,1)} %get-tuple-element.4) | data formatting | bytes 1048576
  64.4 0.0 copy-done
  64.4 0.6 copy.9
Async XLA Ops:
  62.5 1.9 %copy-start = (f32[4,512]{1,0:T(4,128)S(1)}, f32[4,512]{1,0:T(4,128)}, u32[]{:S(2)}) copy-start(f32[4,512]{1,0:T(4,128)} %get-tuple-element.5) | copy-start | bytes 24580

commit v2 on v0

v2 whole, which is shorter than its diff:
```python
import math

import jax
import jax.numpy as jnp
from jax import lax
from jax.experimental import pallas as pl
from jax.experimental.pallas import tpu as pltpu
from jax.sharding import PartitionSpec as P

QH = 4
HD = 128
DOCS = 16
ROWS = 512
PAIR = 2 * ROWS
SHARE = 192
DEPTH = HD + 16
FAR = 1 << 20
HIDE = float(2**20)
LOWEST = -3e38
SCALE = 1.0 / math.sqrt(HD)
TO_TWO = SCALE / math.log(2.0)
MESH = pl.DeviceIdType.MESH

PAIRS = (
    ((0, 3), (3, 0)),
    ((1, 0), (0, 1)),
    ((3, 3), (0, 2)),
    ((2, 0), (3, 1)),
    ((3, 2), (1, 1)),
    ((1, 3), (2, 3)),
    ("pred", (2, 1)),
    ((1, 2), (2, 2)),
)
PLAN = (
    (("swap", "B"), ("high", 3), ("high", 1), ("swap", "A"), ("B", 0, 1), ("B", 0, 3)),
    (("low", 3), ("F", 3), ("F", 1), ("high", 2)),
    (),
    (("A", 3, 3), ("low", 1)),
    (),
    (("B", 3, 3), ("send back",), ("B", 0, 2), ("B", 3, 1), ("A", 1, 3), ("A", 3, 1), ("low", 2)),
    (),
    (("F", 2),),
    (("A", 3, 2), ("B", 1, 1)),
    (("A", 1, 1), ("B", 3, 2), ("B", 1, 3)),
    (),
    (("A", 1, 2), ("A", 2, 3), ("B", 2, 3), ("pred",), ("B", 2, 1)),
    (),
    (("B", 1, 2), ("A", 2, 1)),
    (("A", 2, 2),),
    (("B", 2, 2),),
    (),
)

SLOT = {block: slot for slot, block in enumerate(block for pair in PAIRS for block in pair)}
PRED = SLOT["pred"]
SWAP, OWN = 16, 17
SPARE = {1: 18, 2: 19, 3: 20}
PARTS = {"A": (0, SHARE), "B": (SHARE, ROWS - SHARE), "F": (0, ROWS)}
GOT = {
    name: number
    for number, name in enumerate(
        [("swap", "A"), ("swap", "B"), ("pred",)]
        + [(kind, dx) for kind in ("high", "low") for dx in (1, 2, 3)]
        + [("F", dy) for dy in (1, 2, 3)]
        + [("B", 0, dx) for dx in (1, 2, 3)]
        + [(part, dy, dx) for part in "AB" for dy in (1, 2, 3) for dx in (1, 2, 3)]
    )
}
SENDS = 80


def body(lengths, queries, keys, values, attended, log_mass, kv, qa, acc, top, scores, weights, fade, feats, turned, docs, local, sent, got):
    here = lax.axis_index("ctx")
    z, y, x = here // 16, here // 4 % 4, here % 4
    right, left = z * 16 + y * 4 + (x + 1) % 4, z * 16 + y * 4 + (x + 3) % 4
    down, up = z * 16 + (y + 1) % 4 * 4 + x, z * 16 + (y + 3) % 4 * 4 + x
    other = (1 - z) * 16 + y * 4 + x
    middle_x = (x == 1) | (x == 2)
    middle_y = (y == 1) | (y == 2)
    edge_x = ~middle_x
    high_to = {
        "right": (x < 3) | (z == 0),
        "left": (x == 0) | (z == 0),
        "down": (y < 3) | (z == 0),
        "up": (y == 0) | (z == 0),
    }

    own_copies = [
        pltpu.make_async_copy(keys, kv.at[OWN // 2, 0, pl.ds(ROWS, ROWS)], local.at[0]),
        pltpu.make_async_copy(values, kv.at[OWN // 2, 1, pl.ds(ROWS, ROWS)], local.at[1]),
    ]
    query_copies = [
        pltpu.make_async_copy(
            queries.at[:, pl.ds(head * HD, HD)], qa.at[pl.ds(head * ROWS, ROWS), pl.ds(0, HD)], local.at[2 + head]
        )
        for head in range(QH)
    ]
    for copy in own_copies + query_copies:
        copy.start()
    barrier = pltpu.get_barrier_semaphore()
    for neighbour in (left, right, up, down, other):
        pl.semaphore_signal(barrier, inc=1, device_id={"ctx": neighbour}, device_id_type=MESH)
    pl.semaphore_wait(barrier, 5)
    for copy in own_copies:
        copy.wait()

    def held(slot, part):
        first, rows = PARTS[part]
        start = slot % 2 * ROWS + first
        return kv.at[slot // 2, :, pl.ds(start if isinstance(slot, int) else pl.multiple_of(start, 64), rows)]

    started = {}

    def push(name, part, source, slot, to, signal, when=None):
        def copy():
            return pltpu.make_async_remote_copy(
                src_ref=held(source, part),
                dst_ref=held(slot, part),
                send_sem=sent.at[number],
                recv_sem=got.at[GOT[signal]],
                device_id={"ctx": to},
                device_id_type=MESH,
            )

        number = started[name][0] if name in started else len(started)
        always = name in started or when is None
        started[name] = (number, part, None if always else when)
        if when is None:
            copy().start()
        else:
            pl.when(when)(lambda: copy().start())

    def arrive(signal, part):
        pltpu.make_async_remote_copy(
            src_ref=held(OWN, part),
            dst_ref=held(SWAP, part),
            send_sem=sent.at[0],
            recv_sem=got.at[GOT[signal]],
            device_id={"ctx": other},
            device_id_type=MESH,
        ).wait_recv()

    def row_slot(high, at_z, at_x, dx):
        needed = ((at_x + dx) % 4 < at_x) | (at_z == 0)
        return jnp.where(needed if high else ~needed, SLOT[0, dx], SPARE[dx])

    def across(dx, high):
        source = row_slot(high, z, x, dx)
        for name, to, dy in (("down", down, 3), ("up", up, 1)):
            when = high_to[name] if high else ~high_to[name]
            push((name, dx), "A", source, SLOT[dy, dx], to, ("A", dy, dx), when)

    def first_x(high):
        for name, to, dx in (("right", right, 3), ("left", left, 1)):
            when = high_to[name] if high else ~high_to[name]
            push((name, "first"), "B", OWN if high else SWAP, SLOT[0, dx], to, ("B", 0, dx), when)

    def first_y(high):
        for name, to, dy in (("down", down, 3), ("up", up, 1)):
            when = high_to[name] if high else ~high_to[name]
            push((name, "first"), "F", OWN if high else SWAP, SLOT[dy, 0], to, ("F", dy), when)

    def take(event):
        kind = event[0]
        if kind == "swap":
            arrive(event, event[1])
            if event[1] == "B":
                first_x(False)
            else:
                first_y(False)
        elif kind == "high":
            dx = event[1]
            arrive(event, "A")
            source = row_slot(True, z, x, dx)
            if dx == 3:
                there = row_slot(True, z, (x + 1) % 4, 2)
                push(("turn", 3), "A", source, there, right, ("high", 2), edge_x)
            if dx == 1:
                there = row_slot(True, z, (x + 3) % 4, 2)
                push(("turn", 1), "A", source, there, left, ("high", 2), edge_x)
            push(("swap", dx), "A", source, row_slot(False, 1 - z, x, dx), other, ("low", dx))
            across(dx, True)
        elif kind == "low":
            arrive(event, "A")
            across(event[1], False)
        elif kind == "F":
            dy = event[1]
            arrive(event, "F")
            push(("on", dy, 3), "B", SLOT[dy, 0], SLOT[dy, 3], right, ("B", dy, 3))
            push(("on", dy, 1), "B", SLOT[dy, 0], SLOT[dy, 1], left, ("B", dy, 1))
            if dy == 3:
                push(("far", 3), "F", SLOT[3, 0], SLOT[2, 0], down, ("F", 2), middle_y)
            if dy == 1:
                push(("far", 1), "F", SLOT[1, 0], SLOT[2, 0], up, ("F", 2), middle_y)
        elif kind == "A":
            _, dy, dx = event
            arrive(event, "A")
            if dy != 2:
                push(("far", dy, dx), "A", SLOT[dy, dx], SLOT[2, dx], down if dy == 3 else up, ("A", 2, dx), middle_y)
        elif kind == "B":
            _, dy, dx = event
            arrive(event, "B")
            if dx != 2:
                when = middle_x if dy in (0, 1) else edge_x
                push(("far x", dy, dx), "B", SLOT[dy, dx], SLOT[dy, 2], right if dx == 3 else left, ("B", dy, 2), when)
        elif kind == "send back":
            push(("pred",), "F", jnp.where(x > 0, SLOT[0, 3], SLOT[3, 3]), PRED, other, ("pred",))
        else:
            arrive(event, "F")

    push(("swap", "B"), "B", OWN, SWAP, other, ("swap", "B"))
    push(("swap", "A"), "A", OWN, SWAP, other, ("swap", "A"))
    push(("right", "row"), "A", OWN, row_slot(True, z, (x + 1) % 4, 3), right, ("high", 3))
    push(("left", "row"), "A", OWN, row_slot(True, z, (x + 3) % 4, 1), left, ("high", 1))
    first_x(True)
    first_y(True)

    lane = lax.broadcasted_iota(jnp.int32, (8, 128), 1)
    begins, ends = jnp.full((8, 128), FAR, jnp.int32), jnp.zeros((8, 128), jnp.int32)
    total = jnp.int32(0)
    for doc in range(DOCS):
        begins = jnp.where(lane == doc, total, begins)
        total = total + lengths[doc]
        ends = jnp.where(lane == doc, total, ends)
    docs[0:8] = begins
    docs[8:16] = ends

    def inside(first):
        place = first + lax.broadcasted_iota(jnp.int32, (ROWS, 128), 0)
        return (place >= docs[0:1]) & (place < docs[8:9])

    for copy in query_copies:
        copy.wait()
    hide = jnp.where(inside(here * ROWS), -HIDE, 0.0).astype(jnp.bfloat16)
    for head in range(QH):
        qa[head * ROWS : (head + 1) * ROWS, HD:] = hide
    top[...] = jnp.full(top.shape, -1e30, jnp.float32)
    acc[...] = jnp.zeros(acc.shape, jnp.float32)
    turned[:, HD:, :] = jnp.ones((2, DEPTH - HD, PAIR), jnp.bfloat16)

    def first_of(block):
        if block == OWN:
            return here * ROWS
        if block == SWAP:
            return jnp.where(z == 1, (here - 16) * ROWS, FAR)
        if block == "pred":
            return jnp.where((z == 1) & (here > 16), (here - 17) * ROWS, FAR)
        dy, dx = block
        column = (y + dy) % 4 * 4 + (x + dx) % 4
        before = column < here % 16
        return jnp.where(before, z * 16 + column, jnp.where(z == 1, column, FAR // ROWS)) * ROWS

    def look(block, half):
        feats[half * ROWS : (half + 1) * ROWS] = jnp.where(inside(first_of(block)), 0.0, 1.0).astype(jnp.bfloat16)

    def score(buffer, key_part, columns):
        scores[buffer, 0 : key_part.shape[0]] = lax.dot_general(
            key_part, qa[columns], (((1,), (1,)), ((), ())), preferred_element_type=jnp.float32
        )

    def soften(buffer, width, first_column, reach=None):
        for lanes in range(0, ROWS, 128):
            at = slice(lanes, lanes + 128)
            columns = pl.ds(pl.multiple_of(first_column + lanes, 128), 128)
            raw = scores[buffer, 0:width, at]
            if reach is not None:
                key = lax.broadcasted_iota(jnp.int32, raw.shape, 0)
                raw = jnp.where(key <= lanes + reach + lax.broadcasted_iota(jnp.int32, raw.shape, 1), raw, -1e30)
                scores[buffer, 0:width, at] = raw
            raw = raw.reshape(width // 8, 8, 128)
            most = jnp.max(jnp.max(raw, axis=0), axis=0, keepdims=True)
            before = top[:, columns]
            now = jnp.maximum(before, jnp.broadcast_to(most, (8, 128)))
            top[:, columns] = now
            fade[buffer, :, at] = jnp.exp2((before - now) * TO_TWO)
            for first in range(0, width, 256):
                part = scores[buffer, first : first + 256, at].reshape(32, 8, 128)
                part = jnp.exp2((part - now[None]) * TO_TWO).reshape(256, 128)
                weights[buffer, first : first + 256, at] = part.astype(jnp.bfloat16)

    def mix(buffer, width, value_part, columns):
        more = jnp.dot(value_part, weights[buffer, 0:width], preferred_element_type=jnp.float32)
        faded = acc[:, columns].reshape(DEPTH // 8, 8, ROWS) * fade[buffer][None]
        acc[:, columns] = faded.reshape(DEPTH, ROWS) + more

    def single(number, nothing):
        @pl.when(number == 0)
        def _():
            look(OWN, 0)

        @pl.when(number == 1)
        def _():
            for event in PLAN[0]:
                take(event)
            look(SWAP, 0)

        rows = pl.ds(pl.multiple_of((1 - number) * ROWS, ROWS), ROWS)
        turned[0, 0:HD, 0:ROWS] = kv[SWAP // 2, 1, rows].T
        reach = jnp.where(number == 0, 0, ROWS)
        key_part = jnp.concatenate([kv[SWAP // 2, 0, rows], feats[0:ROWS]], 1)
        value_part = turned[0, :, 0:ROWS]
        columns = [slice(head * ROWS, (head + 1) * ROWS) for head in range(QH)]
        score(0, key_part, columns[0])
        for head in range(QH):
            if head + 1 < QH:
                score((head + 1) % 2, key_part, columns[head + 1])
            if head > 0:
                mix((head - 1) % 2, ROWS, value_part, columns[head - 1])
            soften(head % 2, ROWS, head * ROWS, reach)
        mix(1, ROWS, value_part, columns[QH - 1])
        return nothing

    lax.fori_loop(0, 2, single, 0)

    scores[1] = jnp.full((PAIR, ROWS), LOWEST, jnp.float32)
    weights[0] = jnp.zeros((PAIR, ROWS), jnp.bfloat16)
    fade[0] = jnp.ones((8, ROWS), jnp.float32)

    def stage(number, nothing):
        pair, half = number // 2, number % 2

        def prepare(which):
            for event in PLAN[1 + which]:
                take(event)
            if which % 2 == 0:
                for side in range(2):
                    look(PAIRS[which // 2][side], side)

        for group in range(0, 16, 4):

            @pl.when((number >= group) & (number < group + 4))
            def _():
                for which in range(group, group + 4):
                    if PLAN[1 + which] or which % 2 == 0:
                        pl.when(number == which)(lambda: prepare(which))

        @pl.when(half == 0)
        def _():
            turned[pair % 2, 0:HD] = kv[pair, 1].T

        at = lambda first: pl.ds(pl.multiple_of(first, ROWS), ROWS)
        now_0, now_1 = half * PAIR, half * PAIR + ROWS
        old_0, old_1 = (1 - half) * PAIR, (1 - half) * PAIR + ROWS
        key_part = jnp.concatenate([kv[pair, 0], feats[...]], 1)
        value_part = turned[jnp.maximum(number - 1, 0) // 2 % 2]
        score(0, key_part, at(now_0))
        mix(0, PAIR, value_part, at(old_0))
        soften(1, PAIR, old_1)
        score(1, key_part, at(now_1))
        mix(1, PAIR, value_part, at(old_1))
        soften(0, PAIR, now_0)
        return nothing

    lax.fori_loop(0, 16, stage, 0)

    mix(0, PAIR, turned[1], slice(2 * ROWS, 3 * ROWS))
    soften(1, PAIR, 3 * ROWS)
    mix(1, PAIR, turned[1], slice(3 * ROWS, 4 * ROWS))

    for head in range(QH):
        columns = slice(head * ROWS, (head + 1) * ROWS)
        mass = acc[HD : HD + 1, columns]
        attended[:, head * HD : (head + 1) * HD] = (acc[0:HD, columns] / mass).T.astype(jnp.bfloat16)
        log_mass[head : head + 1, :] = top[0:1, columns] * SCALE + jnp.log(mass)

    for number, part, when in started.values():

        def finish():
            pltpu.make_async_remote_copy(
                src_ref=held(OWN, part),
                dst_ref=held(SWAP, part),
                send_sem=sent.at[number],
                recv_sem=got.at[0],
                device_id={"ctx": other},
                device_id_type=MESH,
            ).wait_send()

        if when is None:
            finish()
        else:
            pl.when(when)(finish)


def on_device(lengths, queries, key_rows, values):
    vmem = pl.BlockSpec(memory_space=pltpu.VMEM)
    hbm = pl.BlockSpec(memory_space=pl.ANY)
    return pl.pallas_call(
        body,
        out_shape=(
            jax.ShapeDtypeStruct((ROWS, QH * HD), jnp.bfloat16),
            jax.ShapeDtypeStruct((QH, ROWS), jnp.float32),
        ),
        in_specs=[pl.BlockSpec(memory_space=pltpu.SMEM), hbm, hbm, hbm],
        out_specs=(vmem, vmem),
        scratch_shapes=[
            pltpu.VMEM((11, 2, PAIR, HD), jnp.bfloat16),
            pltpu.VMEM((QH * ROWS, 2 * HD), jnp.bfloat16),
            pltpu.VMEM((DEPTH, QH * ROWS), jnp.float32),
            pltpu.VMEM((8, QH * ROWS), jnp.float32),
            pltpu.VMEM((2, PAIR, ROWS), jnp.float32),
            pltpu.VMEM((2, PAIR, ROWS), jnp.bfloat16),
            pltpu.VMEM((2, 8, ROWS), jnp.float32),
            pltpu.VMEM((PAIR, HD), jnp.bfloat16),
            pltpu.VMEM((2, DEPTH, PAIR), jnp.bfloat16),
            pltpu.VMEM((16, 128), jnp.int32),
            pltpu.SemaphoreType.DMA((2 + QH,)),
            pltpu.SemaphoreType.DMA((SENDS,)),
            pltpu.SemaphoreType.DMA((len(GOT),)),
        ],
        compiler_params=pltpu.CompilerParams(collective_id=0, has_side_effects=True, vmem_limit_bytes=56 << 20),
    )(lengths, queries, key_rows, values)


def solution(mesh):
    in_specs = (
        P("batch"),
        P(("batch", "ctx"), None),
        P(("batch", "ctx"), None),
        P(("batch", "ctx"), None),
    )
    out_specs = (P(("batch", "ctx"), None), P(None, ("batch", "ctx")))
    step = jax.shard_map(on_device, mesh=mesh, in_specs=in_specs, out_specs=out_specs, check_vma=False)

    def run(*args):
        with jax.sharding.use_abstract_mesh(mesh.abstract_mesh):
            return step(*args)

    return run
```

time: 508 us -> 54.7 us (0.11)
  waiting for transfers between devices: 166 us -> 0 us
  local copies, waits for them, and re-layouts: 144 us -> 2.48 us
  matrix products: 100 us -> 0 us
  other arithmetic: 73.8 us -> 0 us
  Pallas kernels: 0 us -> 51.4 us
  between operations: 14.1 us -> 0.65 us
  loops' own time: 8.29 us -> 0 us
    all_gather x1 -> x0, waiting for transfers between devices: 166 us -> none  [on_device(): lax.all_gather(stacked, 'ctx', axis=1, tiled=True)]
    slice x32 -> x0, local copies, waits for them, and re-layouts: 121 us -> none  [absorb_block(): value_block = lax.dynamic_slice_in_dim(shard_part[1], offset, block_rows, 0)]
    dot_general x256 -> x0, matrix products: 100 us -> none  [the longest x128 51 us: per_query(): jnp.einsum('thd,kd->htk', part_heads, key_block, preferred_element_type=j...]
    pallas_call x0 -> x1, Pallas kernels: none -> 51.4 us  [on_device(): pl.pallas_call(body, out_shape=(jax.ShapeDtypeStruct((ROWS, QH * HD), jnp...]
    reduce_sum x161 -> x0, other arithmetic: 47.2 us -> none  [the longest x128 44.3 us: per_query(): new_sum = run_sum * rescale + jnp.sum(weights, axis=2)]
    dynamic_slice x288 -> x0, local copies, waits for them, and re-layouts: 20.1 us -> none  [the longest x128 9.84 us: per_query(): part_pos = lax.dynamic_slice_in_dim(set_pos, row_start, quarter, 0)]
    and x128 -> x0, other arithmetic: 16.6 us -> none  [per_query(): (part_doc[:, None] == k_doc[None, :]) & (k_pos[None, :] <= part_pos[:, No...]
    another operation x33 -> x0, loops' own time: 8.29 us -> none  [the longest x32 6.59 us: absorb_block(): return lax.fori_loop(0, set_rows // quarter, per_query, carried)]
  transfers between devices with their start and end apart: 1 -> 0, of which waited for: 1 -> 0; matrix products, arithmetic and copies ran while one was open for 0% -> 0% of each run, Pallas kernels for 0% -> 0%
where the time goes in v2:
time: 54.7 us; the launch traced here: 54.5 us
  Pallas kernels  51.4 us (94%)
  local copies, waits for them, and re-layouts  2.48 us (5%)
  between operations  0.65 us (1%)
    pallas_call x1, Pallas kernels, on_device(): pl.pallas_call(body, out_shape=(jax.ShapeDtypeStruct((ROWS, QH * HD), jnp...  51.4 us
    unnamed x4, local copies, waits for them, and re-layouts  2.48 us

profile of v2, /device:TPU:96, one launch (start us, length us, event | category | flops | bytes accessed | tf_op | source)
XLA Modules:
  0.0 54.5 jit_solution(11093868366398676145)
XLA Ops:
  0.6 51.4 %shard_map.59 = (bf16[512,512]{1,0:T(8,128)(2,1)}, f32[4,512]{1,0:T(4,128)}) custom-call(s32[16]{0:T(128)} %lengths.1, bf16[512,512]{1,0:T(8,128)(2,1)} %queries.1, bf16[512,128]{1,0:T(8,128)(2,1)} %keys.1, bf16[512,128]{1,0:T(8,128)(2,1)} %values.1), custom_call_target="tpu_custom_call" | custom-call | tf_op jit(solution)/shard_map/pallas_call | solution.py:387
  52.0 0.0 copy-start
  52.1 1.9 %copy.8 = bf16[512,512]{1,0:T(8,128)(2,1)} copy(bf16[512,512]{1,0:T(8,128)(2,1)} %get-tuple-element.4) | data formatting | bytes 1048576
  53.9 0.0 copy-done
  53.9 0.6 %copy.9 = f32[4,512]{1,0:T(4,128)} copy(f32[4,512]{1,0:T(4,128)S(1)} %copy-done) | data formatting | bytes 16384
Async XLA Ops:
  52.0 1.9 %copy-start = (f32[4,512]{1,0:T(4,128)S(1)}, f32[4,512]{1,0:T(4,128)}, u32[]{:S(2)}) copy-start(f32[4,512]{1,0:T(4,128)} %get-tuple-element.5) | copy-start | bytes 24580

commit v3 on v2

--- a/solution.py
+++ b/solution.py
@@ -69,7 +69,7 @@
 SENDS = 80
 
 
-def body(lengths, queries, keys, values, attended, log_mass, kv, qa, acc, top, scores, weights, fade, feats, turned, docs, local, sent, got):
+def body(lengths, queries, keys, values, attended, log_mass, kv, qa, acc, top, scores, weights, fade, peak, feats, turned, docs, local, sent, got):
     here = lax.axis_index("ctx")
     z, y, x = here // 16, here // 4 % 4, here % 4
     right, left = z * 16 + y * 4 + (x + 1) % 4, z * 16 + y * 4 + (x + 3) % 4
@@ -250,25 +250,26 @@
         before = column < here % 16
         return jnp.where(before, z * 16 + column, jnp.where(z == 1, column, FAR // ROWS)) * ROWS
 
-    def look(block, half):
-        feats[half * ROWS : (half + 1) * ROWS] = jnp.where(inside(first_of(block)), 0.0, 1.0).astype(jnp.bfloat16)
+    def look(block, pair, half):
+        seen = inside(first_of(block))
+        feats[pair, half * ROWS : (half + 1) * ROWS] = jnp.where(seen, 0.0, 1.0).astype(jnp.bfloat16)
 
     def score(buffer, key_part, columns):
-        scores[buffer, 0 : key_part.shape[0]] = lax.dot_general(
-            key_part, qa[columns], (((1,), (1,)), ((), ())), preferred_element_type=jnp.float32
-        )
+        raw = lax.dot_general(key_part, qa[columns], (((1,), (1,)), ((), ())), preferred_element_type=jnp.float32)
+        scores[buffer, 0 : key_part.shape[0]] = raw
+        peak[buffer] = jnp.max(raw.reshape(-1, 8, ROWS), axis=0)
 
     def soften(buffer, width, first_column, reach=None):
         for lanes in range(0, ROWS, 128):
             at = slice(lanes, lanes + 128)
             columns = pl.ds(pl.multiple_of(first_column + lanes, 128), 128)
-            raw = scores[buffer, 0:width, at]
+            raw = scores[buffer, 0:width, at] if reach is not None else None
             if reach is not None:
                 key = lax.broadcasted_iota(jnp.int32, raw.shape, 0)
                 raw = jnp.where(key <= lanes + reach + lax.broadcasted_iota(jnp.int32, raw.shape, 1), raw, -1e30)
                 scores[buffer, 0:width, at] = raw
-            raw = raw.reshape(width // 8, 8, 128)
-            most = jnp.max(jnp.max(raw, axis=0), axis=0, keepdims=True)
+            most = peak[buffer, :, at] if raw is None else jnp.max(raw.reshape(width // 8, 8, 128), axis=0)
+            most = jnp.max(most, axis=0, keepdims=True)
             before = top[:, columns]
             now = jnp.maximum(before, jnp.broadcast_to(most, (8, 128)))
             top[:, columns] = now
@@ -283,21 +284,10 @@
         faded = acc[:, columns].reshape(DEPTH // 8, 8, ROWS) * fade[buffer][None]
         acc[:, columns] = faded.reshape(DEPTH, ROWS) + more
 
-    def single(number, nothing):
-        @pl.when(number == 0)
-        def _():
-            look(OWN, 0)
-
-        @pl.when(number == 1)
-        def _():
-            for event in PLAN[0]:
-                take(event)
-            look(SWAP, 0)
-
-        rows = pl.ds(pl.multiple_of((1 - number) * ROWS, ROWS), ROWS)
-        turned[0, 0:HD, 0:ROWS] = kv[SWAP // 2, 1, rows].T
-        reach = jnp.where(number == 0, 0, ROWS)
-        key_part = jnp.concatenate([kv[SWAP // 2, 0, rows], feats[0:ROWS]], 1)
+    def single(slot, reach):
+        rows = pl.ds(slot % 2 * ROWS, ROWS)
+        turned[0, 0:HD, 0:ROWS] = kv[slot // 2, 1, rows].T
+        key_part = jnp.concatenate([kv[slot // 2, 0, rows], feats[len(PAIRS), rows]], 1)
         value_part = turned[0, :, 0:ROWS]
         columns = [slice(head * ROWS, (head + 1) * ROWS) for head in range(QH)]
         score(0, key_part, columns[0])
@@ -308,13 +298,21 @@
                 mix((head - 1) % 2, ROWS, value_part, columns[head - 1])
             soften(head % 2, ROWS, head * ROWS, reach)
         mix(1, ROWS, value_part, columns[QH - 1])
-        return nothing
-
-    lax.fori_loop(0, 2, single, 0)
+
+    look(OWN, len(PAIRS), OWN % 2)
+    single(OWN, 0)
+    look(SWAP, len(PAIRS), SWAP % 2)
+    for number, pair in enumerate(PAIRS):
+        for half in range(2):
+            look(pair[half], number, half)
+    for event in PLAN[0]:
+        take(event)
+    single(SWAP, None)
 
     scores[1] = jnp.full((PAIR, ROWS), LOWEST, jnp.float32)
     weights[0] = jnp.zeros((PAIR, ROWS), jnp.bfloat16)
     fade[0] = jnp.ones((8, ROWS), jnp.float32)
+    peak[1] = jnp.full((8, ROWS), LOWEST, jnp.float32)
 
     def stage(number, nothing):
         pair, half = number // 2, number % 2
@@ -322,16 +320,13 @@
         def prepare(which):
             for event in PLAN[1 + which]:
                 take(event)
-            if which % 2 == 0:
-                for side in range(2):
-                    look(PAIRS[which // 2][side], side)
 
         for group in range(0, 16, 4):
 
             @pl.when((number >= group) & (number < group + 4))
             def _():
                 for which in range(group, group + 4):
-                    if PLAN[1 + which] or which % 2 == 0:
+                    if PLAN[1 + which]:
                         pl.when(number == which)(lambda: prepare(which))
 
         @pl.when(half == 0)
@@ -341,14 +336,19 @@
         at = lambda first: pl.ds(pl.multiple_of(first, ROWS), ROWS)
         now_0, now_1 = half * PAIR, half * PAIR + ROWS
         old_0, old_1 = (1 - half) * PAIR, (1 - half) * PAIR + ROWS
-        key_part = jnp.concatenate([kv[pair, 0], feats[...]], 1)
-        value_part = turned[jnp.maximum(number - 1, 0) // 2 % 2]
-        score(0, key_part, at(now_0))
-        mix(0, PAIR, value_part, at(old_0))
-        soften(1, PAIR, old_1)
-        score(1, key_part, at(now_1))
-        mix(1, PAIR, value_part, at(old_1))
-        soften(0, PAIR, now_0)
+
+        @pl.when(here >= 0)
+        def _():
+            soften(1, PAIR, old_1)
+            score(0, jnp.concatenate([kv[pair, 0], feats[pair]], 1), at(now_0))
+            mix(0, PAIR, turned[jnp.maximum(number - 1, 0) // 2 % 2], at(old_0))
+
+        @pl.when(here < 32)
+        def _():
+            soften(0, PAIR, now_0)
+            score(1, jnp.concatenate([kv[pair, 0], feats[pair]], 1), at(now_1))
+            mix(1, PAIR, turned[jnp.maximum(number - 1, 0) // 2 % 2], at(old_1))
+
         return nothing
 
     lax.fori_loop(0, 16, stage, 0)
@@ -383,7 +383,7 @@
 
 def on_device(lengths, queries, key_rows, values):
     vmem = pl.BlockSpec(memory_space=pltpu.VMEM)
-    hbm = pl.BlockSpec(memory_space=pl.ANY)
+    hbm = pl.BlockSpec(memory_space=pltpu.HBM)
     return pl.pallas_call(
         body,
         out_shape=(
@@ -400,7 +400,8 @@
             pltpu.VMEM((2, PAIR, ROWS), jnp.float32),
             pltpu.VMEM((2, PAIR, ROWS), jnp.bfloat16),
             pltpu.VMEM((2, 8, ROWS), jnp.float32),
-            pltpu.VMEM((PAIR, HD), jnp.bfloat16),
+            pltpu.VMEM((2, 8, ROWS), jnp.float32),
+            pltpu.VMEM((len(PAIRS) + 1, PAIR, HD), jnp.bfloat16),
             pltpu.VMEM((2, DEPTH, PAIR), jnp.bfloat16),
             pltpu.VMEM((16, 128), jnp.int32),
             pltpu.SemaphoreType.DMA((2 + QH,)),

time: 54.7 us -> 51.4 us (0.940)
  Pallas kernels: 51.4 us -> 48.1 us
    pallas_call x1, Pallas kernels: 51.4 us -> 48.1 us  [on_device(): pl.pallas_call(body, out_shape=(jax.ShapeDtypeStruct((ROWS, QH * HD), jnp...]
where the time goes in v3:
time: 51.4 us; the launch traced here: 51.3 us
  Pallas kernels  48.1 us (94%)
  local copies, waits for them, and re-layouts  2.48 us (5%)
  between operations  0.65 us (1%)
    pallas_call x1, Pallas kernels, on_device(): pl.pallas_call(body, out_shape=(jax.ShapeDtypeStruct((ROWS, QH * HD), jnp...  48.1 us
    unnamed x4, local copies, waits for them, and re-layouts  2.48 us

profile of v3, /device:TPU:96, one launch (start us, length us, event | category | flops | bytes accessed | tf_op | source)
XLA Modules:
  0.0 51.3 jit_solution(4832266043173904787)
XLA Ops:
  0.6 48.1 %shard_map.59 = (bf16[512,512]{1,0:T(8,128)(2,1)}, f32[4,512]{1,0:T(4,128)}) custom-call(s32[16]{0:T(128)} %lengths.1, bf16[512,512]{1,0:T(8,128)(2,1)} %queries.1, bf16[512,128]{1,0:T(8,128)(2,1)} %keys.1, bf16[512,128]{1,0:T(8,128)(2,1)} %values.1), custom_call_target="tpu_custom_call" | custom-call | tf_op jit(solution)/shard_map/pallas_call | solution.py:387
  48.8 0.0 copy-start
  48.8 1.9 %copy.8 = bf16[512,512]{1,0:T(8,128)(2,1)} copy(bf16[512,512]{1,0:T(8,128)(2,1)} %get-tuple-element.4) | data formatting | bytes 1048576
  50.7 0.0 copy-done
  50.7 0.6 %copy.9 = f32[4,512]{1,0:T(4,128)} copy(f32[4,512]{1,0:T(4,128)S(1)} %copy-done) | data formatting | bytes 16384
Async XLA Ops:
  48.8 1.9 %copy-start = (f32[4,512]{1,0:T(4,128)S(1)}, f32[4,512]{1,0:T(4,128)}, u32[]{:S(2)}) copy-start(f32[4,512]{1,0:T(4,128)} %get-tuple-element.5) | copy-start | bytes 24580

commit v4 on v3

--- a/solution.py
+++ b/solution.py
@@ -360,7 +360,7 @@
     for head in range(QH):
         columns = slice(head * ROWS, (head + 1) * ROWS)
         mass = acc[HD : HD + 1, columns]
-        attended[:, head * HD : (head + 1) * HD] = (acc[0:HD, columns] / mass).T.astype(jnp.bfloat16)
+        attended[:, head * HD : (head + 1) * HD] = (acc[0:HD, columns] * (1.0 / mass)).astype(jnp.bfloat16).T
         log_mass[head : head + 1, :] = top[0:1, columns] * SCALE + jnp.log(mass)
 
     for number, part, when in started.values():

time: 51.4 us -> 51.4 us (level)
  no operation moved by 1% of the time
where the time goes in v4:
time: 51.4 us; the launch traced here: 51.2 us
  Pallas kernels  48.1 us (94%)
  local copies, waits for them, and re-layouts  2.48 us (5%)
  between operations  0.65 us (1%)
    pallas_call x1, Pallas kernels, on_device(): pl.pallas_call(body, out_shape=(jax.ShapeDtypeStruct((ROWS, QH * HD), jnp...  48.1 us
    unnamed x4, local copies, waits for them, and re-layouts  2.48 us

profile of v4, /device:TPU:96, one launch (start us, length us, event | category | flops | bytes accessed | tf_op | source)
XLA Modules:
  0.0 51.2 jit_solution(5582204877006076501)
XLA Ops:
  0.6 48.1 %shard_map.59 = (bf16[512,512]{1,0:T(8,128)(2,1)}, f32[4,512]{1,0:T(4,128)}) custom-call(s32[16]{0:T(128)} %lengths.1, bf16[512,512]{1,0:T(8,128)(2,1)} %queries.1, bf16[512,128]{1,0:T(8,128)(2,1)} %keys.1, bf16[512,128]{1,0:T(8,128)(2,1)} %values.1), custom_call_target="tpu_custom_call" | custom-call | tf_op jit(solution)/shard_map/pallas_call | solution.py:387
  48.8 0.0 copy-start
  48.8 1.9 %copy.8 = bf16[512,512]{1,0:T(8,128)(2,1)} copy(bf16[512,512]{1,0:T(8,128)(2,1)} %get-tuple-element.4) | data formatting | bytes 1048576
  50.6 0.0 copy-done
  50.6 0.6 %copy.9 = f32[4,512]{1,0:T(4,128)} copy(f32[4,512]{1,0:T(4,128)S(1)} %copy-done) | data formatting | bytes 16384
Async XLA Ops:
  48.8 1.9 %copy-start = (f32[4,512]{1,0:T(4,128)S(1)}, f32[4,512]{1,0:T(4,128)}, u32[]{:S(2)}) copy-start(f32[4,512]{1,0:T(4,128)} %get-tuple-element.5) | copy-start | bytes 24580
